TPU v7x, 256 devices: a whole 4x4x8 slice. The times are simulated.
256 devices in a mesh: row: 32 (over x_lo, z, core), col: 8 (over x_hi, y).
Axes of the slice: x: 4 (x_hi: 2, x_lo: 2; x = x_hi * 2 + x_lo), y: 4, z: 8, core: 2. Of those that a mesh axis runs over, the one named last changes fastest.
Arguments:
- features: bfloat16 [65536, 512], P(('row', 'col')), may hold values from -6 to 6
- weight: bfloat16 [512, 512], replicated, may hold values from -0.25 to 0.25
- out_grad: bfloat16 [65536, 512], P(('row', 'col')), may hold values from -6 to 6
- relu_mask: int32 [65536, 512], P(('row', 'col')), may hold values 0 or 1
- adjacency_tiles: bfloat16 [49152, 128, 128], P(('row', 'col')), may hold values from -0.1875 to 0.1875
- tile_rows: int32 [49152], P(('row', 'col')), may hold values from 0 to 15
- tile_cols: int32 [49152], P(('row', 'col')), may hold values from 0 to 63
- tile_count: int32 [256], P(('row', 'col')), may hold values from 24 to 192, as said below
Outputs:
- input_grad: bfloat16 [65536, 512], P(('row', 'col'))
- weight_grad: float32 [512, 512], replicated
Inputs may be any that keep to these rules, and one draw needn't show every extreme that they name: Only the first tile_count slots of a device are live; some device has all 192 slots live in every draw.
All inputs are finite; a program needn't handle non-finite values. No bound on the sum of `relu_mask` on one device may be relied on, other than what follows from the above.
Results may differ from a plain program's by a relative error of at most 0.0049.
Values may be sent and summed in bfloat16 or wider, within the bound.
No kernel may reach another device: no remote copies, remote signals or barrier semaphores. Data moves between devices by JAX's collectives and lax.ppermute only.
A program may use at most 128 MiB of HBM per device.

v0:
```python
import math
import jax
import jax.numpy as jnp
from jax import lax
from jax.sharding import PartitionSpec as P

GROUP = 8


def sweep(running, tile_set, block_set, col_set, row_set, live_count, group_size, turns):

    def advance(turn_index, carried):
        first_slot = turn_index * group_size
        part_tiles = lax.dynamic_slice_in_dim(tile_set, first_slot, group_size, 0)
        part_cols = lax.dynamic_slice_in_dim(col_set, first_slot, group_size, 0)
        part_rows = lax.dynamic_slice_in_dim(row_set, first_slot, group_size, 0)
        part_blocks = jnp.take(block_set, part_rows, axis=0)
        slot_ids = first_slot + jnp.arange(group_size, dtype=jnp.int32)
        kept = jnp.where(
            (slot_ids < live_count)[:, None, None], part_tiles, jnp.zeros_like(part_tiles)
        )
        terms = jnp.einsum("tij,tif->tjf", kept, part_blocks, preferred_element_type=jnp.float32)
        return carried.at[part_cols].add(terms)

    return lax.fori_loop(0, turns, advance, running)


def shards(
    features, weight, out_grad, relu_mask, adjacency_tiles, tile_rows, tile_cols, tile_count
):
    tile_size = adjacency_tiles.shape[1]
    feature_width = features.shape[1]
    col_slots = lax.axis_size("row") * (features.shape[0] // tile_size)
    masked_grad = out_grad * relu_mask.astype(jnp.bfloat16)
    panel = lax.all_gather(masked_grad, "col", axis=0, tiled=True)
    grad_blocks = panel.reshape(-1, tile_size, feature_width)
    own_count = tile_count[0]
    slot_sets = (adjacency_tiles, grad_blocks, tile_cols, tile_rows, own_count, True)
    running = jnp.zeros((col_slots, tile_size, feature_width), jnp.float32)
    tile_set, block_set, col_set, row_set, live_count, keep_dead = slot_sets
    turns = tile_set.shape[0] // GROUP
    running = sweep(running, tile_set, block_set, col_set, row_set, live_count, GROUP, turns)
    summed = lax.psum_scatter(
        running.reshape(col_slots * tile_size, feature_width),
        "row",
        scatter_dimension=0,
        tiled=True,
    )
    node_grad = summed.astype(jnp.bfloat16)
    input_grad = lax.dot_general(
        node_grad, weight, (((1,), (1,)), ((), ())), preferred_element_type=jnp.float32
    ).astype(jnp.bfloat16)
    partial_weight = lax.dot_general(
        features, node_grad, (((0,), (0,)), ((), ())), preferred_element_type=jnp.float32
    )
    node_total = features.shape[0] * lax.axis_size("row") * lax.axis_size("col")
    weight_grad = lax.psum(partial_weight, ("row", "col")) * (1.0 / math.sqrt(node_total))
    return (input_grad, weight_grad)


def solution(mesh):
    return jax.shard_map(
        shards,
        mesh=mesh,
        in_specs=(
            P(("row", "col"), None),
            P(),
            P(("row", "col"), None),
            P(("row", "col"), None),
            P(("row", "col"), None, None),
            P(("row", "col")),
            P(("row", "col")),
            P(("row", "col")),
        ),
        out_specs=(P(("row", "col"), None), P()),
        check_vma=False,
    )
```

profile of v0, /device:TPU:2, one launch (start us, length us, event | category | flops | bytes accessed | tf_op | source)
XLA Modules:
  0.0 763.1 jit_solution(5273142124928129784)
XLA Ops:
  9.2 62.6 %all-gather.2.cloned.1.call-done = bf16[2048,512]{1,0:T(8,128)(2,1)} async-done(((bf16[256,512]{1,0:T(8,128)(2,1)}), bf16[2048,512]{1,0:T(8,128)(2,1)}) %all-gather.2.cloned.1.call-update) | async-done | bytes 2097168 | tf_op jit(solution)/shard_map/all_gather | solution.py:35
  71.8 7.9 %broadcast_in_dim.55 = f32[64,128,512]{2,1,0:T(8,128)} broadcast(f32[]{:T(128)} %constant.74.clone.1), dimensions={} | broadcast | bytes 16777220 | tf_op jit(solution)/shard_map/broadcast_in_dim | solution.py:39
  79.7 269.1 %while.13 = (s32[]{:T(128)}, f32[64,128,512]{2,1,0:T(8,128)}, s32[192]{0:T(256)S(1)}, s32[]{:T(128)}, bf16[192,128,128]{2,1,0:T(8,128)(2,1)}, /*index=5*/s32[192...) while((s32[]{:T(128)}, f32[64,128,512]{2,1,0:T(8,128)}, ...), condition=%wide.region_2.3_spmd, body=%wide.region_0.2_spmd.sunk | while | flops 135398496 | bytes 12849583 | solution.py:25
  81.7 3.2 gather_fusion
  86.6 4.4 scatter_fusion
  92.9 3.2 gather_fusion
  97.8 4.4 scatter_fusion
  104.2 3.2 gather_fusion
  109.1 4.3 scatter_fusion
  115.3 3.2 gather_fusion
  120.2 4.4 scatter_fusion
  126.6 3.2 gather_fusion
  131.5 4.4 scatter_fusion
  137.8 3.2 gather_fusion
  142.7 4.4 scatter_fusion
  149.1 3.2 gather_fusion
  154.0 4.3 scatter_fusion
  160.3 3.2 gather_fusion
  165.2 4.3 scatter_fusion
  171.4 3.2 gather_fusion
  176.3 4.4 scatter_fusion
  182.7 3.2 gather_fusion
  187.6 4.3 scatter_fusion
  193.8 3.2 gather_fusion
  198.7 4.3 scatter_fusion
  205.0 3.2 gather_fusion
  209.9 4.4 scatter_fusion
  216.3 3.2 gather_fusion
  221.2 4.3 scatter_fusion
  227.5 3.2 gather_fusion
  232.4 4.4 scatter_fusion
  238.8 3.2 gather_fusion
  243.7 4.3 scatter_fusion
  249.9 3.2 gather_fusion
  254.8 4.3 scatter_fusion
  261.1 3.2 gather_fusion
  265.9 4.4 scatter_fusion
  272.3 3.2 gather_fusion
  277.2 4.3 scatter_fusion
  283.5 3.2 gather_fusion
  288.4 4.4 scatter_fusion
  299.7 4.3 scatter_fusion
  310.9 4.3 scatter_fusion
  322.1 4.3 scatter_fusion
  333.2 4.4 scatter_fusion
  344.5 4.4 scatter_fusion
  348.9 143.5 %reduce-scatter.2.cloned.1.call-done = f32[256,512]{1,0:T(8,128)} async-done(((f32[8192,512]{1,0:T(8,128)}), f32[256,512]{1,0:T(8,128)}) %reduce-scatter.2.cloned.1.call-update) | async-done | bytes 524304 | tf_op jit(solution)/shard_map/reduce_scatter | solution.py:43
  496.9 257.0 %all-reduce.2.cloned.1.call-done = f32[512,512]{0,1:T(8,128)} async-done(((f32[512,512]{0,1:T(8,128)}), f32[512,512]{0,1:T(8,128)}) %all-reduce.2.cloned.1.call-update) | async-done | bytes 1048592 | tf_op jit(solution)/shard_map/psum | solution.py:57
  (168 shorter events, 113.1 us)
Async XLA Ops:
  7.2 487.6 %copy-start = (bf16[512,512]{1,0:T(8,128)(2,1)S(1)}, bf16[512,512]{1,0:T(8,128)(2,1)}, u32[]{:S(2)}) copy-start(bf16[512,512]{1,0:T(8,128)(2,1)} %param.11) | copy-start | bytes 1572868
  7.2 64.7 %all-gather.2.cloned.1.call-start = ((), (), s32[]{:S(2)}) async-start(), calls=%async_computation.1 | async-start | bytes 2359296 | tf_op jit(solution)/shard_map/all_gather | solution.py:35
  9.2 483.2 %reduce-scatter.2.cloned.1.call-start = ((), (), s32[]{:S(2)}) async-start(), calls=%async_computation.2 | async-start | bytes 17301504 | tf_op jit(solution)/shard_map/reduce_scatter | solution.py:43
  71.8 7.9 %copy-start.2 = (s32[192]{0:T(256)S(1)}, s32[192]{0:T(256)}, u32[]{:S(2)}) copy-start(s32[192]{0:T(256)} %param.15) | copy-start | bytes 2308
  71.8 7.9 %copy-start.3 = (s32[192]{0:T(256)S(1)}, s32[192]{0:T(256)}, u32[]{:S(2)}) copy-start(s32[192]{0:T(256)} %param.16) | copy-start | bytes 2308
  348.8 143.6 %copy-start.1 = (bf16[256,512]{1,0:T(8,128)(2,1)S(1)}, bf16[256,512]{1,0:T(8,128)(2,1)}, u32[]{:S(2)}) copy-start(bf16[256,512]{1,0:T(8,128)(2,1)} %param.10) | copy-start | bytes 786436
  348.9 405.0 %all-reduce.2.cloned.1.call-start = ((), (), s32[]{:S(2)}) async-start(), calls=%async_computation.3 | async-start | bytes 2097152 | tf_op jit(solution)/shard_map/psum | solution.py:57
Sparse Core Ops, SparseCore 0:
  11.2 60.5 all-gather.1
  349.0 143.3 reduce-scatter.1
  498.4 255.4 all-reduce.1
where the time goes:
time: 767 us; the launch traced here: 763 us
  waiting for transfers between devices  463 us (60%)
  other arithmetic  127 us (17%)
  local copies, waits for them, and re-layouts  113 us (15%)
  matrix products  45.6 us (6%)
  between operations  13.8 us (2%)
    psum x1, waiting for transfers between devices, shards(): lax.psum(partial_weight, ('row', 'col')) * (1.0 / math.sqrt(node_total))  257 us
    reduce_scatter x1, waiting for transfers between devices, shards(): lax.psum_scatter(running.reshape(col_slots * tile_size, feature_width), '...  143 us
    scatter-add x24, other arithmetic, advance(): return carried.at[part_cols].add(terms)  104 us
    gather x24, local copies, waits for them, and re-layouts, advance(): part_blocks = jnp.take(block_set, part_rows, axis=0)  76.2 us
    all_gather x1, waiting for transfers between devices, shards(): panel = lax.all_gather(masked_grad, 'col', axis=0, tiled=True)  62.6 us
    dot_general x24, matrix products, advance(): jnp.einsum('tij,tif->tjf', kept, part_blocks, preferred_element_type=jnp....  41.1 us
    dynamic_slice x48, local copies, waits for them, and re-layouts, advance(): part_tiles = lax.dynamic_slice_in_dim(tile_set, first_slot, group_size, 0)  27.7 us
    and x24, other arithmetic, advance(): part_blocks = jnp.take(block_set, part_rows, axis=0)  17.4 us
  transfers between devices with their start and end apart: 3, of which 3 were waited for; matrix products, arithmetic and copies ran while one was open for 0% of the time, Pallas kernels for 0%

commit v1 on v0

--- a/solution.py
+++ b/solution.py
@@ -1,3 +1,4 @@
+import functools
 import math
 import jax
 import jax.numpy as jnp
@@ -5,6 +6,15 @@
 from jax.sharding import PartitionSpec as P
 
 GROUP = 8
+
+
+def _recast_face(base_x, row_axis, which_dim):
+    t_next = tuple((base_x for _ in range(lax.axis_size(row_axis))))
+    all_values = lax.all_to_all(jnp.stack(t_next, axis=0), row_axis, 0, 0)
+    return jnp.concatenate(all_values, axis=which_dim)
+
+
+turn_axis_part = functools.partial(_recast_face, row_axis="col", which_dim=0)
 
 
 def sweep(running, tile_set, block_set, col_set, row_set, live_count, group_size, turns):
@@ -32,7 +42,7 @@
     feature_width = features.shape[1]
     col_slots = lax.axis_size("row") * (features.shape[0] // tile_size)
     masked_grad = out_grad * relu_mask.astype(jnp.bfloat16)
-    panel = lax.all_gather(masked_grad, "col", axis=0, tiled=True)
+    panel = turn_axis_part(masked_grad)
     grad_blocks = panel.reshape(-1, tile_size, feature_width)
     own_count = tile_count[0]
     slot_sets = (adjacency_tiles, grad_blocks, tile_cols, tile_rows, own_count, True)

time: 767 us -> 740 us (0.965)
  waiting for transfers between devices: 463 us -> 430 us
    all_gather x1 -> x0, waiting for transfers between devices: 62.6 us -> none  [shards(): panel = lax.all_gather(masked_grad, 'col', axis=0, tiled=True)]
    all_to_all x0 -> x1, waiting for transfers between devices: none -> 26.5 us  [_recast_face(): all_values = lax.all_to_all(jnp.stack(t_next, axis=0), row_axis, 0, 0)]
where the time goes in v1:
time: 740 us; the launch traced here: 737 us
  waiting for transfers between devices  430 us (58%)
  other arithmetic  126 us (17%)
  local copies, waits for them, and re-layouts  115 us (16%)
  matrix products  45.6 us (6%)
  between operations  14.1 us (2%)
    psum x1, waiting for transfers between devices, shards(): lax.psum(partial_weight, ('row', 'col')) * (1.0 / math.sqrt(node_total))  257 us
    reduce_scatter x1, waiting for transfers between devices, shards(): lax.psum_scatter(running.reshape(col_slots * tile_size, feature_width), '...  146 us
    scatter-add x24, other arithmetic, advance(): return carried.at[part_cols].add(terms)  104 us
    gather x24, local copies, waits for them, and re-layouts, advance(): part_blocks = jnp.take(block_set, part_rows, axis=0)  76.2 us
    dot_general x24, matrix products, advance(): jnp.einsum('tij,tif->tjf', kept, part_blocks, preferred_element_type=jnp....  41.1 us
    dynamic_slice x48, local copies, waits for them, and re-layouts, advance(): part_tiles = lax.dynamic_slice_in_dim(tile_set, first_slot, group_size, 0)  27.7 us
    all_to_all x1, waiting for transfers between devices, _recast_face(): all_values = lax.all_to_all(jnp.stack(t_next, axis=0), row_axis, 0, 0)  26.5 us
    and x24, other arithmetic, advance(): part_blocks = jnp.take(block_set, part_rows, axis=0)  17.4 us
  transfers between devices with their start and end apart: 3, of which 3 were waited for; matrix products, arithmetic and copies ran while one was open for 0% of the time, Pallas kernels for 0%

profile of v1, /device:TPU:2, one launch (start us, length us, event | category | flops | bytes accessed | tf_op | source)
XLA Modules:
  0.0 736.5 jit_solution(4451299421205433960)
XLA Ops:
  9.9 6.0 all-to-all-start
  16.0 26.5 %all-to-all-done = bf16[8,256,512]{2,1,0:T(8,128)(2,1)} async-done(((bf16[8,256,512]{2,1,0:T(8,128)(2,1)}), bf16[8,256,512]{2,1,0:T(8,128)(2,1)}, u32[]{:S(2)}, u32[]{:S(2)}) %all-to-all-start) | async-done | bytes 2097184 | tf_op jit(solution)/shard_map/all_to_all | solution.py:13
  42.5 7.9 %broadcast_in_dim.55 = f32[64,128,512]{2,1,0:T(8,128)} broadcast(f32[]{:T(128)} %constant.74.clone.1), dimensions={} | broadcast | bytes 16777220 | tf_op jit(solution)/shard_map/broadcast_in_dim | solution.py:49
  50.4 269.0 %while.13 = (s32[]{:T(128)}, f32[64,128,512]{2,1,0:T(8,128)}, s32[192]{0:T(256)S(1)}, s32[]{:T(128)}, bf16[192,128,128]{2,1,0:T(8,128)(2,1)}, /*index=5*/s32[192...) while((s32[]{:T(128)}, f32[64,128,512]{2,1,0:T(8,128)}, ...), condition=%wide.region_2.3_spmd, body=%wide.region_0.2_spmd.sunk | while | flops 135398496 | bytes 12849583 | solution.py:35
  52.3 3.2 gather_fusion
  57.2 4.4 scatter_fusion
  63.6 3.2 gather_fusion
  68.5 4.4 scatter_fusion
  74.8 3.2 gather_fusion
  79.7 4.3 scatter_fusion
  86.0 3.2 gather_fusion
  90.9 4.4 scatter_fusion
  97.3 3.2 gather_fusion
  102.2 4.4 scatter_fusion
  108.5 3.2 gather_fusion
  113.4 4.4 scatter_fusion
  119.8 3.2 gather_fusion
  124.7 4.3 scatter_fusion
  130.9 3.2 gather_fusion
  135.8 4.3 scatter_fusion
  142.1 3.2 gather_fusion
  147.0 4.4 scatter_fusion
  153.4 3.2 gather_fusion
  158.3 4.2 scatter_fusion
  164.5 3.2 gather_fusion
  169.4 4.3 scatter_fusion
  175.6 3.2 gather_fusion
  180.5 4.4 scatter_fusion
  186.8 3.2 gather_fusion
  191.7 4.3 scatter_fusion
  198.0 3.2 gather_fusion
  202.9 4.4 scatter_fusion
  209.3 3.2 gather_fusion
  214.2 4.3 scatter_fusion
  220.4 3.2 gather_fusion
  225.3 4.3 scatter_fusion
  231.6 3.2 gather_fusion
  236.5 4.4 scatter_fusion
  242.9 3.2 gather_fusion
  247.8 4.4 scatter_fusion
  259.0 4.4 scatter_fusion
  270.3 4.3 scatter_fusion
  281.4 4.3 scatter_fusion
  292.6 4.3 scatter_fusion
  303.8 4.4 scatter_fusion
  315.0 4.3 scatter_fusion
  319.4 146.1 %reduce-scatter.2.cloned.1.call-done = f32[256,512]{1,0:T(8,128)} async-done(((f32[8192,512]{1,0:T(8,128)}), f32[256,512]{1,0:T(8,128)}) %reduce-scatter.2.cloned.1.call-update) | async-done | bytes 524304 | tf_op jit(solution)/shard_map/reduce_scatter | solution.py:53
  470.0 257.1 %all-reduce.2.cloned.1.call-done = f32[512,512]{0,1:T(8,128)} async-done(((f32[512,512]{0,1:T(8,128)}), f32[512,512]{0,1:T(8,128)}) %all-reduce.2.cloned.1.call-update) | async-done | bytes 1048592 | tf_op jit(solution)/shard_map/psum | solution.py:67
  (168 shorter events, 117.1 us)
Async XLA Ops:
  7.2 460.7 %copy-start = (bf16[512,512]{1,0:T(8,128)(2,1)S(1)}, bf16[512,512]{1,0:T(8,128)(2,1)}, u32[]{:S(2)}) copy-start(bf16[512,512]{1,0:T(8,128)(2,1)} %param.11) | copy-start | bytes 1572868
  9.9 32.6 %all-to-all-start = ((bf16[8,256,512]{2,1,0:T(8,128)(2,1)}), bf16[8,256,512]{2,1,0:T(8,128)(2,1)}, u32[]{:S(2)}, u32[]{:S(2)}) async-start(bf16[8,256,512]{2,1,0:T(8,128)(2,1)} %stack.2), calls=%async_computation | async-start | bytes 4194304 | tf_op jit(solution)/shard_map/all_to_all | solution.py:13
  16.0 449.6 %reduce-scatter.2.cloned.1.call-start = ((), (), s32[]{:S(2)}) async-start(), calls=%async_computation.2 | async-start | bytes 17301504 | tf_op jit(solution)/shard_map/reduce_scatter | solution.py:53
  42.5 7.9 %copy-start.2 = (s32[192]{0:T(256)S(1)}, s32[192]{0:T(256)}, u32[]{:S(2)}) copy-start(s32[192]{0:T(256)} %param.15) | copy-start | bytes 2308
  42.5 7.9 %copy-start.3 = (s32[192]{0:T(256)S(1)}, s32[192]{0:T(256)}, u32[]{:S(2)}) copy-start(s32[192]{0:T(256)} %param.16) | copy-start | bytes 2308
  319.3 146.2 %copy-start.1 = (bf16[256,512]{1,0:T(8,128)(2,1)S(1)}, bf16[256,512]{1,0:T(8,128)(2,1)}, u32[]{:S(2)}) copy-start(bf16[256,512]{1,0:T(8,128)(2,1)} %param.10) | copy-start | bytes 786436
  319.4 407.7 %all-reduce.2.cloned.1.call-start = ((), (), s32[]{:S(2)}) async-start(), calls=%async_computation.3 | async-start | bytes 2097152 | tf_op jit(solution)/shard_map/psum | solution.py:67
Sparse Core Ops, SparseCore 0:
  319.5 146.0 reduce-scatter.1
  471.6 255.4 all-reduce.1
